TPU v7x, 32 devices: a whole 2x2x4 slice. The times are simulated.
32 devices in a mesh: groups: 2 (over x), patch: 8 (over z, y), section: 2 (over core).
Axes of the slice: x: 2, y: 2, z: 4, core: 2. Of those that a mesh axis runs over, the one named last changes fastest.
Arguments:
- hidden_in: bfloat16 [6144, 3072], P(('groups', 'patch')), parts along dimension 0, may hold values from -6 to 6
- text_rows: bfloat16 [256, 3072], P('groups', 'patch'), parts along dimension 0, may hold values from -6 to 6
- mod_table: float32 [50, 2, 5, 3072], P(None, 'section'), may hold values from -3 to 3
- timestep: int32 [2], P('groups'), parts along dimension 0, may hold values from 0 to 49
- w_query: bfloat16 [2, 3072, 1536], P('section', 'patch'), may hold values from -0.109375 to 0.109375
- w_out: bfloat16 [2, 1536, 3072], P('section', 'patch'), may hold values from -1.25 to 1.25
- w_text: bfloat16 [2, 3072, 3072], P('section', 'patch'), may hold values from -0.109375 to 0.109375
- stale_kv: bfloat16 [2, 6144, 3072], P('section', ('groups', 'patch')), parts along dimension 1, may hold values from -450 to 450
- mask_blocks: int32 [48, 4], P(('groups', 'patch')), parts along dimension 0, may hold values from 0 to 23, as said below
- counts: int32 [48], P(('groups', 'patch')), parts along dimension 0, may hold values from 1 to 4, as said below
Outputs:
- hidden_out: bfloat16 [2, 6144, 3072], P('section', ('groups', 'patch')), parts along dimension 1
There are 2 independent parts, one for each index of `groups`. A program takes and returns all parts, laid end to end along the dimension named above; an argument that names none is the same for every part. Nothing has to cross between parts.
Inputs may be any that keep to these rules, and one draw needn't show every extreme that they name: `mask_blocks`: row b lists 4 different block numbers, b itself first; every one is a block stored on the same patch device as block b or on the device just before or after it (384 tokens a device, blocks of 128 tokens). Only the first counts[b] entries of row b of mask_blocks are used; some block has 4.
All inputs are finite; a program needn't handle non-finite values.
Results may differ from a plain program's by a relative error of at most 0.037.
Values may be sent and summed in bfloat16 or wider, within the bound.
A program may use at most 128 MiB of HBM per device.

v0:
```python
import jax
import jax.numpy as jnp
from jax import lax
from jax.sharding import PartitionSpec as P

HD = 128
BLK = 128


EPSILON = 1e-06


def with_halo(block, sides, width):
    for axis, dim in sides:
        count = lax.axis_size(axis)
        forward = [(i, i + 1) for i in range(count - 1)]
        backward = [(target, source) for source, target in forward]
        low = lax.ppermute(
            lax.slice_in_dim(block, block.shape[dim] - width, None, axis=dim), axis, forward
        )
        high = lax.ppermute(lax.slice_in_dim(block, 0, width, axis=dim), axis, backward)
        block = jnp.concatenate([low, block, high], axis=dim)
    return block


def shifted(value, axis, by):
    size = lax.axis_size(axis)
    pairs = [(i, i + by) for i in range(size) if 0 <= i + by < size]
    return lax.ppermute(value, axis, pairs)


def layer_norm(values):
    values = values.astype(jnp.float32)
    center = values - jnp.mean(values, axis=-1, keepdims=True)
    spread = jnp.mean(center * center, axis=-1, keepdims=True)
    return center * lax.rsqrt(spread + EPSILON)


def attend_block(block_query, image_pairs, text_pairs, live_count):
    inner = block_query.shape[1]
    heads = inner // HD
    length = block_query.shape[0]
    joined = jnp.concatenate([text_pairs, image_pairs], axis=0)
    slot = jnp.arange(image_pairs.shape[0], dtype=jnp.int32) // length
    live = jnp.concatenate([jnp.ones((text_pairs.shape[0],), dtype=jnp.bool_), slot < live_count])
    keys = joined[:, :inner].reshape(-1, heads, HD)
    values = joined[:, inner:].reshape(-1, heads, HD)
    query_heads = block_query.reshape(length, heads, HD)
    scores = jnp.einsum(
        "qhd,khd->hqk", query_heads, keys, preferred_element_type=jnp.float32
    ) * HD ** (-0.5)
    scores = jnp.where(live[None, None, :], scores, -1e30)
    peak = jnp.max(scores, axis=-1, keepdims=True)
    raised = jnp.exp(scores - peak)
    probs = (raised / jnp.sum(raised, axis=-1, keepdims=True)).astype(jnp.bfloat16)
    mixed = jnp.einsum("hqk,khd->qhd", probs, values, preferred_element_type=jnp.float32)
    return mixed.reshape(length, inner).astype(jnp.bfloat16)


def local(
    hidden_in, text_rows, mod_table, timestep, w_query, w_out, w_text, stale_kv, mask_blocks, counts
):
    patch_id = lax.axis_index("patch")
    section_id = lax.axis_index("section")
    width = text_rows.shape[1]
    per_device = hidden_in.shape[0] // BLK
    modulation = lax.dynamic_index_in_dim(mod_table, timestep[0], 0, keepdims=False)[0]
    text_shift = lax.dynamic_slice_in_dim(modulation[3], patch_id * width, width, 0)
    text_scale = lax.dynamic_slice_in_dim(modulation[4], patch_id * width, width, 0)
    conditioned = (text_rows.astype(jnp.float32) * (1.0 + text_scale) + text_shift).astype(
        jnp.bfloat16
    )
    partial_pairs = jnp.dot(conditioned, w_text[0], preferred_element_type=jnp.float32)
    text_pairs = lax.psum(partial_pairs, "patch").astype(jnp.bfloat16)
    local_pairs = stale_kv[0]
    tokens = local_pairs.shape[0]
    rimmed = with_halo(local_pairs, (("patch", 0),), tokens)
    stale_blocks = rimmed.reshape(3 * per_device, BLK, local_pairs.shape[1])
    local_index = mask_blocks - (patch_id - 1) * per_device
    query_whole, out_whole = (
        lax.all_gather(w_query, "patch", axis=1, tiled=True),
        lax.all_gather(w_out, "patch", axis=1, tiled=True),
    )
    query_whole = query_whole[0]
    out_whole = out_whole[0]

    def layer_block(state, slot):
        normed = (layer_norm(state) * (1.0 + modulation[1]) + modulation[0]).astype(jnp.bfloat16)
        query = jnp.dot(normed, query_whole, preferred_element_type=jnp.float32)
        query = query.astype(jnp.bfloat16)
        chosen = lax.dynamic_index_in_dim(local_index, slot, 0, keepdims=False)
        live_count = lax.dynamic_index_in_dim(counts, slot, 0, keepdims=False)
        image_pairs = jnp.take(stale_blocks, chosen, axis=0).reshape(-1, stale_blocks.shape[2])
        attended = attend_block(query, image_pairs, text_pairs, live_count)
        projected = jnp.dot(attended, out_whole, preferred_element_type=jnp.float32)
        return (state.astype(jnp.float32) + modulation[2] * projected).astype(jnp.bfloat16)

    def tick(index, carry):
        results, inbox = carry
        micro = index - section_id
        slot = jnp.clip(micro, 0, per_device - 1)
        own_rows = lax.dynamic_slice_in_dim(
            hidden_in, jnp.minimum(index, per_device - 1) * BLK, BLK, 0
        )
        state = jnp.where(section_id == 0, own_rows, inbox)
        fresh = layer_block(state, slot)
        usable = (micro >= 0) & (micro < per_device)
        updated = lax.dynamic_update_slice_in_dim(results, fresh, slot * BLK, 0)
        results = jnp.where(usable, updated, results)
        inbox = shifted(fresh, "section", 1)
        return (results, inbox)

    start_rows = jnp.zeros((BLK, hidden_in.shape[1]), jnp.bfloat16)
    results, inbox = lax.fori_loop(0, per_device + 1, tick, (jnp.zeros_like(hidden_in), start_rows))
    return results[None]


def solution(mesh):
    in_specs = (
        P(("groups", "patch"), None),
        P("groups", "patch"),
        P(None, "section", None, None),
        P("groups"),
        P("section", "patch", None),
        P("section", "patch", None),
        P("section", "patch", None),
        P("section", ("groups", "patch"), None),
        P(("groups", "patch"), None),
        P(("groups", "patch")),
    )
    out_specs = P("section", ("groups", "patch"), None)
    return jax.shard_map(local, mesh=mesh, in_specs=in_specs, out_specs=out_specs, check_vma=False)
```

profile of v0, /device:TPU:5, one launch (start us, length us, event | category | flops | bytes accessed | tf_op | source)
XLA Modules:
  0.0 585.3 jit_solution(13573750182443311422)
XLA Ops:
  8.0 1.9 collective-permute-start.2
  9.9 4.3 collective-permute-start.1
  16.5 1.7 fusion.30
  18.2 211.9 %all-reduce.2 = bf16[128,3072]{1,0:T(8,128)(2,1)S(1)} all-reduce(f32[128,3072]{1,0:T(8,128)} %fusion.30), channel_id=1, replica_groups=mesh['groups'=2,'patch'=8,'section'=2] {'patch'}, use_global_device_ids=true, to_apply=%region_0.1 | all-reduce | flops 393216 | bytes 2359296 | tf_op jit(solution)/shard_map/psum | solution.py:74
  230.5 6.5 %pad_maximum_fusion.1 = bf16[1152,3072]{1,0:T(8,128)(2,1)} fusion(bf16[384,3072]{1,0:T(8,128)(2,1)} %collective-permute-done.2, bf16[384,3072]{1,0:T(8,128)(2,1)} %bitcast.91, bf16[384,3072]{1,0:T(8,128)(2,1)} %collective-permute-done.1), kind=kLoop, calls=%fused_computation.55 | loop fusion | flops 21233664 | bytes 14155776 | tf_op jit(solution)/shard_map/concatenate | solution.py:22
  237.0 27.9 %all-gather.3.cloned.1.call-done = bf16[1,3072,1536]{2,1,0:T(8,128)(2,1)} async-done(((bf16[1,384,1536]{2,1,0:T(8,128)(2,1)}), bf16[1,3072,1536]{2,1,0:T(8,128)(2,1)}) %all-gather.3.cloned.1.call-update) | async-done | bytes 9437200 | tf_op jit(solution)/shard_map/all_gather | solution.py:81
  264.9 138.3 %all-gather.5.cloned.1.call-done = bf16[1,1536,3072]{2,1,0:T(8,128)(2,1)} async-done(((bf16[1,192,3072]{2,1,0:T(8,128)(2,1)}), bf16[1,1536,3072]{2,1,0:T(8,128)(2,1)}) %all-gather.5.cloned.1.call-update) | async-done | bytes 9437200 | tf_op jit(solution)/shard_map/all_gather | solution.py:82
  403.3 1.7 broadcast_in_dim.79
  404.9 171.9 %while.17 = (s32[]{:T(128)}, bf16[384,3072]{1,0:T(8,128)(2,1)}, bf16[128,3072]{1,0:T(8,128)(2,1)S(1)}, s32[]{:T(128)}, pred[]{:T(512)}, /*index=5*/bf16[384,3072...) while((s32[]{:T(128)}, bf16[384,3072]{1,0:T(8,128)(2,1)}, ...), condition=%wide.region_6.7_spmd, body=%wide.region_1.6_spmd.sunk | while | flops 2942051584 | bytes 117313912 | solution.py:114
  406.2 1.5 convert_reduce_fusion.2
  408.0 5.1 convolution_convert_fusion.2
  413.4 5.4 gather_fusion
  418.8 4.7 copy.27
  423.5 2.2 broadcast_select_fusion.2
  425.7 2.9 pad_maximum_fusion.3
  428.6 5.0 fusion.69
  433.6 3.8 fusion.70
  439.5 2.6 select_dynamic-update-slice_fusion.2
  444.8 3.4 collective-permute-done
  449.4 1.5 convert_reduce_fusion.2
  451.2 5.1 convolution_convert_fusion.2
  456.6 5.4 gather_fusion
  461.9 4.7 copy.27
  466.6 2.2 broadcast_select_fusion.2
  468.8 2.9 pad_maximum_fusion.3
  471.7 5.0 fusion.69
  476.8 3.8 fusion.70
  482.7 2.6 select_dynamic-update-slice_fusion.2
  487.9 3.1 collective-permute-done
  494.1 5.1 convolution_convert_fusion.2
  499.5 5.4 gather_fusion
  504.8 4.7 copy.27
  509.5 2.2 broadcast_select_fusion.2
  511.7 2.9 pad_maximum_fusion.3
  514.6 5.0 fusion.69
  519.7 3.8 fusion.70
  525.5 2.6 select_dynamic-update-slice_fusion.2
  530.8 3.1 collective-permute-done
  537.0 5.1 convolution_convert_fusion.2
  542.4 5.4 gather_fusion
  547.7 4.7 copy.27
  552.4 2.2 broadcast_select_fusion.2
  554.6 2.9 pad_maximum_fusion.3
  557.5 5.0 fusion.69
  562.6 3.8 fusion.70
  568.4 2.6 select_dynamic-update-slice_fusion.2
  573.7 3.1 collective-permute-done
  576.8 1.7 copy-done.1
  (119 shorter events, 32.8 us)
Async XLA Ops:
  6.5 9.9 %copy-start = (bf16[1,384,3072]{2,1,0:T(8,128)(2,1)S(1)}, bf16[1,384,3072]{2,1,0:T(8,128)(2,1)}, u32[]{:S(2)}) copy-start(bf16[1,384,3072]{2,1,0:T(8,128)(2,1)} %param.18) | copy-start | bytes 7077892
  6.5 9.9 %copy-start.4 = (bf16[128,384]{1,0:T(8,128)(2,1)S(1)}, bf16[128,384]{1,0:T(8,128)(2,1)}, u32[]{:S(2)}) copy-start(bf16[128,384]{1,0:T(8,128)(2,1)} %param.13) | copy-start | bytes 294916
  6.5 258.4 %all-gather.3.cloned.1.call-start = ((), (), s32[]{:S(2)}) async-start(), calls=%async_computation | async-start | bytes 10616832 | tf_op jit(solution)/shard_map/all_gather | solution.py:81
  7.3 395.9 %all-gather.5.cloned.1.call-start = ((), (), s32[]{:S(2)}) async-start(), calls=%async_computation.1 | async-start | bytes 10616832 | tf_op jit(solution)/shard_map/all_gather | solution.py:82
  8.0 222.5 %collective-permute-start.2 = (bf16[384,3072]{1,0:T(8,128)(2,1)}, bf16[384,3072]{1,0:T(8,128)(2,1)}, u32[]{:S(2)}, u32[]{:S(2)}) collective-permute-start(bf16[384,3072]{1,0:T(8,128)(2,1)} %bitcast.89), channel_id=1, source_target_pairs={{2,0},{4,2},{6,4},{8,6},{10,8},{12,10},{14,12},{3,1},{5,3},{7,5},{... | collective-permute-start | bytes 7077896 | tf_op jit(solution)/shard_map/ppermute | solution.py:21
  9.9 220.6 %collective-permute-start.1 = (bf16[384,3072]{1,0:T(8,128)(2,1)}, bf16[384,3072]{1,0:T(8,128)(2,1)}, u32[]{:S(2)}, u32[]{:S(2)}) collective-permute-start(bf16[384,3072]{1,0:T(8,128)(2,1)} %bitcast.90), channel_id=1, source_target_pairs={{0,2},{2,4},{4,6},{6,8},{8,10},{10,12},{12,14},{1,3},{3,5},{5,7},{... | collective-permute-start | bytes 7077896 | tf_op jit(solution)/shard_map/ppermute | solution.py:18
  18.2 212.3 %copy-start.5 = (s32[3,4]{1,0:T(4,128)S(1)}, s32[3,4]{1,0:T(4,128)}, u32[]{:S(2)}) copy-start(s32[3,4]{1,0:T(4,128)} %param.20) | copy-start | bytes 148
  237.0 167.9 %copy-start.6 = (s32[3]{0:T(128)S(1)}, s32[3]{0:T(128)}, u32[]{:S(2)}) copy-start(s32[3]{0:T(128)} %param.21) | copy-start | bytes 40
  428.6 8.8 %slice-start = ((s8[9437184]{0:T(1024)(128)(4,1)}), s8[1048576]{0:T(1024)(128)(4,1)S(1)}, s32[]{:S(2)}) async-start(s8[9437184]{0:T(1024)(128)(4,1)} %bitcast.81), calls=%async_computation.2 | async-start | bytes 2097152 | tf_op jit(solution)/shard_map/while
  433.6 3.9 slice-start.1
  433.6 5.2 slice-start.2
  433.6 5.9 %copy-start.2 = (bf16[384,3072]{1,0:T(8,128)(2,1)S(1)}, bf16[384,3072]{1,0:T(8,128)(2,1)}, u32[]{:S(2)}) copy-start(bf16[384,3072]{1,0:T(8,128)(2,1)} %get-tuple-element.486) | copy-start | bytes 7077892 | tf_op jit(solution)/shard_map/while
  442.1 1.4 copy-start.3
  443.5 4.6 collective-permute-start
  471.7 8.8 %slice-start = ((s8[9437184]{0:T(1024)(128)(4,1)}), s8[1048576]{0:T(1024)(128)(4,1)S(1)}, s32[]{:S(2)}) async-start(s8[9437184]{0:T(1024)(128)(4,1)} %bitcast.81), calls=%async_computation.2 | async-start | bytes 2097152 | tf_op jit(solution)/shard_map/while
  476.8 3.9 slice-start.1
  476.8 5.2 slice-start.2
  476.8 5.9 %copy-start.2 = (bf16[384,3072]{1,0:T(8,128)(2,1)S(1)}, bf16[384,3072]{1,0:T(8,128)(2,1)}, u32[]{:S(2)}) copy-start(bf16[384,3072]{1,0:T(8,128)(2,1)} %get-tuple-element.486) | copy-start | bytes 7077892 | tf_op jit(solution)/shard_map/while
  485.2 1.4 copy-start.3
  486.6 4.4 collective-permute-start
  514.6 8.8 %slice-start = ((s8[9437184]{0:T(1024)(128)(4,1)}), s8[1048576]{0:T(1024)(128)(4,1)S(1)}, s32[]{:S(2)}) async-start(s8[9437184]{0:T(1024)(128)(4,1)} %bitcast.81), calls=%async_computation.2 | async-start | bytes 2097152 | tf_op jit(solution)/shard_map/while
  519.7 3.9 slice-start.1
  519.7 5.2 slice-start.2
  519.7 5.9 %copy-start.2 = (bf16[384,3072]{1,0:T(8,128)(2,1)S(1)}, bf16[384,3072]{1,0:T(8,128)(2,1)}, u32[]{:S(2)}) copy-start(bf16[384,3072]{1,0:T(8,128)(2,1)} %get-tuple-element.486) | copy-start | bytes 7077892 | tf_op jit(solution)/shard_map/while
  528.1 1.4 copy-start.3
  529.5 4.4 collective-permute-start
  557.5 8.8 %slice-start = ((s8[9437184]{0:T(1024)(128)(4,1)}), s8[1048576]{0:T(1024)(128)(4,1)S(1)}, s32[]{:S(2)}) async-start(s8[9437184]{0:T(1024)(128)(4,1)} %bitcast.81), calls=%async_computation.2 | async-start | bytes 2097152 | tf_op jit(solution)/shard_map/while
  562.6 3.9 slice-start.1
  562.6 5.2 slice-start.2
  562.6 5.9 %copy-start.2 = (bf16[384,3072]{1,0:T(8,128)(2,1)S(1)}, bf16[384,3072]{1,0:T(8,128)(2,1)}, u32[]{:S(2)}) copy-start(bf16[384,3072]{1,0:T(8,128)(2,1)} %get-tuple-element.486) | copy-start | bytes 7077892 | tf_op jit(solution)/shard_map/while
  571.0 1.4 copy-start.3
  572.4 4.4 collective-permute-start
  576.8 1.7 copy-start.1
Sparse Core Ops, SparseCore 0:
  9.5 255.3 all-gather.2
  267.1 136.0 all-gather.4
where the time goes:
time: 589 us; the launch traced here: 585 us
  blocking collectives  212 us (36%)
  waiting for transfers between devices  180 us (31%)
  matrix products  67.8 us (12%)
  local copies, waits for them, and re-layouts  62.2 us (11%)
  other arithmetic  37.3 us (6%)
  between operations  14.2 us (2%)
  starting transfers between devices  11.3 us (2%)
    psum x1, blocking collectives, local(): text_pairs = lax.psum(partial_pairs, 'patch').astype(jnp.bfloat16)  212 us
    all_gather x1, waiting for transfers between devices, local(): lax.all_gather(w_out, 'patch', axis=1, tiled=True)  138 us
    gather x8, local copies, waits for them, and re-layouts, layer_block(): jnp.take(stale_blocks, chosen, axis=0).reshape(-1, stale_blocks.shape[2])  40.2 us
    all_gather x1, waiting for transfers between devices, local(): lax.all_gather(w_query, 'patch', axis=1, tiled=True)  27.9 us
    dot_general x4, matrix products, layer_block(): query = jnp.dot(normed, query_whole, preferred_element_type=jnp.float32)  20.5 us
    sub x4, matrix products, attend_block(): raised = jnp.exp(scores - peak)  20.2 us
    dot_general x4, matrix products, attend_block(): jnp.einsum('hqk,khd->qhd', probs, values, preferred_element_type=jnp.floa...  15.1 us
    while x40, local copies, waits for them, and re-layouts  13.9 us
  transfers between devices with their start and end apart: 8, of which 6 were waited for; matrix products, arithmetic and copies ran while one was open for 2% of the time, Pallas kernels for 0%

commit v1 on v0

v1 whole, which is shorter than its diff:
```python
import functools

import jax
import jax.numpy as jnp
from jax import lax
from jax.experimental import pallas as pl
from jax.experimental.pallas import tpu as pltpu
from jax.sharding import PartitionSpec as P

HD = 128
BLK = 128
EPSILON = 1e-06
MESH = pl.DeviceIdType.MESH
ROWS = 16


def exclusive_rows(rows):
    return max(rows * 5 // 12 // ROWS, 1) * ROWS


def gather_kernel(
    n, wq, wo, kv, part, wq_all, wo_all, kv_rim, text,
    sums, total, ring_send, ring_recv, mate_send, mate_recv,
    rim_send, rim_recv, text_send, text_recv, share_send, share_recv, local_sem,
):
    me = lax.axis_index("patch")
    group = lax.axis_index("groups")
    parity = lax.rem(group, 2)
    mate = group + 1 - 2 * parity
    half = n // 2
    odd = lax.rem(me, 2)
    place = (1 - odd) * lax.div(me, 2) + odd * (n - 1 - lax.div(me, 2))

    def at(position):
        position = lax.rem(position + n, n)
        high = lax.div(position, half)
        return (1 - high) * 2 * position + high * (2 * (n - 1 - position) + 1)

    right, left = at(place + 1), at(place - 1)
    peers = [lax.rem(me + step, n) for step in range(1, n)]

    barrier = pltpu.get_barrier_semaphore()
    for peer in peers:
        pl.semaphore_signal(barrier, inc=1, device_id={"patch": peer}, device_id_type=MESH)
    pl.semaphore_signal(barrier, inc=1, device_id={"groups": mate}, device_id_type=MESH)
    pl.semaphore_wait(barrier, n)

    flows = (
        (wq, wq_all, -1, half),
        (wq, wq_all, 1, half - 1),
        (wo, wo_all, -1, half - 1),
        (wo, wo_all, 1, half),
    )

    def remote(src, dst, send, recv, target):
        return pltpu.make_async_remote_copy(
            src_ref=src, dst_ref=dst, send_sem=send, recv_sem=recv,
            device_id=target, device_id_type=MESH,
        )

    def rows_of(own):
        rows = own.shape[0]
        apart = exclusive_rows(rows)
        return rows, apart, rows - apart

    def span(start, size):
        return pl.ds(pl.multiple_of(start, ROWS), size)

    def ring(flow, hop, received=False):
        own, every, way, _ = flows[flow]
        _, apart, keep = rows_of(own)
        shard = at(place + way * (hop if received else hop - 1))
        window = span(parity * apart, keep)
        dst = every.at[shard, window]
        src = own.at[window] if hop == 1 and not received else dst
        target = {"patch": right if way < 0 else left}
        return remote(src, dst, ring_send.at[flow, hop - 1], ring_recv.at[flow, hop - 1], target)

    def across(flow, hop, received=False):
        own, every, way, _ = flows[flow]
        _, apart, keep = rows_of(own)
        shard = at(place + way * hop)
        side = 1 - parity if received else parity
        ref = every.at[shard, span(side * keep, apart)]
        return remote(ref, ref, mate_send.at[flow, hop - 1], mate_recv.at[flow, hop - 1], {"groups": mate})

    blocks = kv.shape[0] // BLK

    def rim(side, block, received=False):
        window = pl.ds(block * BLK, BLK)
        slot = side if not received else side
        target = {"patch": me + 1 if side == 0 else me - 1}
        return remote(
            kv.at[window], kv_rim.at[slot, window],
            rim_send.at[side, block], rim_recv.at[side, block], target,
        )

    def rim_start(block):
        @pl.when(me < n - 1)
        def _():
            rim(0, block).start()

        @pl.when(me > 0)
        def _():
            rim(1, block).start()

    def scatter(step, received=False):
        peer = lax.rem(me + step, n)
        source = lax.rem(me + n - step, n)
        return remote(
            part.at[peer], sums.at[source if received else me],
            text_send.at[step - 1], text_recv.at[step - 1], {"patch": peer},
        )

    def share(step, received=False):
        peer = lax.rem(me + step, n)
        source = lax.rem(me + n - step, n)
        slot = source if received else me
        return remote(
            text.at[slot], text.at[slot],
            share_send.at[step - 1], share_recv.at[step - 1], {"patch": peer},
        )

    for flow in range(4):
        ring(flow, 1).start()
    own_sum = pltpu.make_async_copy(part.at[me], sums.at[me], local_sem.at[0])
    own_sum.start()
    for step in range(1, n):
        scatter(step).start()

    started = 0
    for hop in range(1, half + 1):
        if started < blocks:
            rim_start(started)
            started += 1
        for flow in range(4):
            if hop <= flows[flow][3]:
                ring(flow, hop, True).wait_recv()
                if hop < flows[flow][3]:
                    ring(flow, hop + 1).start()
                across(flow, hop).start()
        if hop == 1:
            own_sum.wait()
            for step in range(1, n):
                scatter(step, True).wait_recv()
            total[...] = jnp.sum(sums[...], axis=0).astype(total.dtype)
            keep_sum = pltpu.make_async_copy(total, text.at[me], local_sem.at[1])
            keep_sum.start()
            keep_sum.wait()
            for step in range(1, n):
                share(step).start()
    for block in range(started, blocks):
        rim_start(block)

    for flow in range(4):
        for hop in range(1, flows[flow][3] + 1):
            across(flow, hop, True).wait_recv()
            across(flow, hop).wait_send()
            ring(flow, hop).wait_send()
    for step in range(1, n):
        scatter(step).wait_send()
        share(step).wait_send()
        share(step, True).wait_recv()
    for block in range(blocks):
        @pl.when(me < n - 1)
        def _():
            rim(0, block).wait_send()
            rim(1, block).wait_recv()

        @pl.when(me > 0)
        def _():
            rim(1, block).wait_send()
            rim(0, block).wait_recv()


def gather_all(n, wq, wo, kv, part):
    half = n // 2
    blocks = kv.shape[0] // BLK
    anywhere = pl.BlockSpec(memory_space=pl.ANY)
    dma = pltpu.SemaphoreType.DMA
    return pl.pallas_call(
        functools.partial(gather_kernel, n),
        out_shape=(
            jax.ShapeDtypeStruct((n,) + wq.shape, wq.dtype),
            jax.ShapeDtypeStruct((n,) + wo.shape, wo.dtype),
            jax.ShapeDtypeStruct((2,) + kv.shape, kv.dtype),
            jax.ShapeDtypeStruct(part.shape, jnp.bfloat16),
        ),
        in_specs=[anywhere] * 4,
        out_specs=(anywhere,) * 4,
        scratch_shapes=[
            pltpu.VMEM(part.shape, jnp.float32),
            pltpu.VMEM(part.shape[1:], jnp.bfloat16),
            dma((4, half)), dma((4, half)), dma((4, half)), dma((4, half)),
            dma((2, blocks)), dma((2, blocks)),
            dma((n - 1,)), dma((n - 1,)), dma((n - 1,)), dma((n - 1,)),
            dma((2,)),
        ],
        compiler_params=pltpu.CompilerParams(collective_id=0, has_side_effects=True),
        name="gather_all",
    )(wq, wo, kv, part)


def layer_kernel(
    scalars, chosen, counts, state, modulation, wq, wo, wq_all, wo_all, kv, kv_rim, text, out,
    wq_full, wo_full, joined, normed, query, mixed, wq_sem, wo_sem, kv_sem, text_sem,
):
    n = wq_all.shape[0]
    me = scalars[0]
    tokens, width = state.shape
    blocks = tokens // BLK
    inner = query.shape[1]
    heads = inner // HD
    spread = chosen.shape[1]
    keys = joined.shape[1]
    lead = keys - spread * BLK

    def fetch(own, every, full, sem):
        rows = own.shape[0]
        for shard in range(n):
            target = full.at[pl.ds(shard * rows, rows)]

            @pl.when(me == shard)
            def _():
                pltpu.make_async_copy(own, target, sem.at[shard]).start()

            @pl.when(me != shard)
            def _():
                pltpu.make_async_copy(every.at[shard], target, sem.at[shard]).start()

    def fetched(own, full, sem):
        rows = own.shape[0]
        for shard in range(n):
            pltpu.make_async_copy(own, full.at[pl.ds(shard * rows, rows)], sem.at[shard]).wait()

    fetch(wq, wq_all, wq_full, wq_sem)
    for block in range(blocks):
        pltpu.make_async_copy(text, joined.at[block, pl.ds(0, lead)], text_sem.at[block]).start()
        for slot in range(spread):
            pick = chosen[block, slot] - (me - 1) * blocks
            home = lax.div(pick, blocks)
            row = pl.multiple_of(lax.rem(pick, blocks) * BLK, BLK)
            target = joined.at[block, pl.ds(lead + slot * BLK, BLK)]

            @pl.when(home == 1)
            def _():
                pltpu.make_async_copy(kv.at[pl.ds(row, BLK)], target, kv_sem.at[block, slot]).start()

            @pl.when(home != 1)
            def _():
                pltpu.make_async_copy(
                    kv_rim.at[lax.div(home, 2), pl.ds(row, BLK)], target, kv_sem.at[block, slot]
                ).start()
    fetch(wo, wo_all, wo_full, wo_sem)

    step = 16

    @pl.loop(0, tokens // step)
    def _(index):
        window = pl.ds(pl.multiple_of(index * step, step), step)
        values = state[window, :].astype(jnp.float32)
        center = values - jnp.mean(values, axis=-1, keepdims=True)
        variance = jnp.mean(center * center, axis=-1, keepdims=True)
        scaled = center * lax.rsqrt(variance + EPSILON)
        normed[window, :] = (
            scaled * (1.0 + modulation[1:2, :]) + modulation[0:1, :]
        ).astype(normed.dtype)

    fetched(wq, wq_full, wq_sem)
    tile = 256

    @pl.loop(0, inner // tile)
    def _(index):
        window = pl.ds(pl.multiple_of(index * tile, tile), tile)
        query[:, window] = jnp.dot(
            normed[...], wq_full[:, window], preferred_element_type=jnp.float32
        ).astype(query.dtype)

    for block in range(blocks):
        pltpu.make_async_copy(text, joined.at[block, pl.ds(0, lead)], text_sem.at[block]).wait()
        for slot in range(spread):
            target = joined.at[block, pl.ds(lead + slot * BLK, BLK)]
            pltpu.make_async_copy(kv.at[pl.ds(0, BLK)], target, kv_sem.at[block, slot]).wait()

    together = 4 if heads % 4 == 0 else 1
    bunches = heads // together

    @pl.loop(0, blocks * bunches)
    def _(index):
        block = lax.div(index, bunches)
        bunch = lax.rem(index, bunches)
        rows = pl.ds(pl.multiple_of(block * BLK, BLK), BLK)
        limit = lead + counts[block] * BLK
        live = lax.broadcasted_iota(jnp.int32, (BLK, keys), 1) < limit
        for one in range(together):
            start = bunch * (together * HD) + one * HD
            columns = pl.ds(pl.multiple_of(start, HD), HD)
            beyond = pl.ds(pl.multiple_of(inner + start, HD), HD)
            scores = lax.dot_general(
                query[rows, columns], joined[block, :, columns], (((1,), (1,)), ((), ())),
                preferred_element_type=jnp.float32,
            )
            scores = jnp.where(live, scores, -1e30)
            peak = jnp.max(scores, axis=-1, keepdims=True)
            raised = jnp.exp((scores - peak) * HD ** (-0.5))
            whole = jnp.sum(raised, axis=-1, keepdims=True)
            share = jnp.dot(
                raised.astype(jnp.bfloat16), joined[block, :, beyond],
                preferred_element_type=jnp.float32,
            )
            mixed[rows, columns] = (share / whole).astype(mixed.dtype)

    fetched(wo, wo_full, wo_sem)

    @pl.loop(0, width // tile)
    def _(index):
        window = pl.ds(pl.multiple_of(index * tile, tile), tile)
        projected = jnp.dot(mixed[...], wo_full[:, window], preferred_element_type=jnp.float32)
        out[:, window] = (
            state[:, window].astype(jnp.float32) + modulation[2:3, window] * projected
        ).astype(out.dtype)


def layer(scalars, chosen, counts, state, modulation, wq, wo, wq_all, wo_all, kv, kv_rim, text):
    n = wq_all.shape[0]
    tokens, width = state.shape
    blocks = tokens // BLK
    inner = wq.shape[1]
    spread = chosen.shape[1]
    smem = pl.BlockSpec(memory_space=pltpu.SMEM)
    vmem = pl.BlockSpec(memory_space=pltpu.VMEM)
    anywhere = pl.BlockSpec(memory_space=pl.ANY)
    dma = pltpu.SemaphoreType.DMA
    return pl.pallas_call(
        layer_kernel,
        out_shape=jax.ShapeDtypeStruct(state.shape, state.dtype),
        in_specs=[smem] * 3 + [vmem] * 2 + [anywhere] * 7,
        out_specs=vmem,
        scratch_shapes=[
            pltpu.VMEM((n * wq.shape[0], inner), wq.dtype),
            pltpu.VMEM((n * wo.shape[0], width), wo.dtype),
            pltpu.VMEM((blocks, text.shape[0] + spread * BLK, kv.shape[1]), kv.dtype),
            pltpu.VMEM(state.shape, jnp.bfloat16),
            pltpu.VMEM((tokens, inner), jnp.bfloat16),
            pltpu.VMEM((tokens, inner), jnp.bfloat16),
            dma((n,)), dma((n,)), dma((blocks, spread)), dma((blocks,)),
        ],
        compiler_params=pltpu.CompilerParams(vmem_limit_bytes=60 * 2**20),
        name="layer",
    )(scalars, chosen, counts, state, modulation, wq, wo, wq_all, wo_all, kv, kv_rim, text)


def local(
    hidden_in, text_rows, mod_table, timestep, w_query, w_out, w_text, stale_kv, mask_blocks, counts
):
    patch_id = lax.axis_index("patch")
    section_id = lax.axis_index("section")
    n = lax.axis_size("patch")
    width = text_rows.shape[1]
    modulation = lax.dynamic_index_in_dim(mod_table, timestep[0], 0, keepdims=False)[0]
    text_shift = lax.dynamic_slice_in_dim(modulation[3], patch_id * width, width, 0)
    text_scale = lax.dynamic_slice_in_dim(modulation[4], patch_id * width, width, 0)
    conditioned = (text_rows.astype(jnp.float32) * (1.0 + text_scale) + text_shift).astype(
        jnp.bfloat16
    )
    partial_pairs = jnp.dot(conditioned, w_text[0], preferred_element_type=jnp.float32)
    wq, wo, kv = w_query[0], w_out[0], stale_kv[0]
    wq_all, wo_all, kv_rim, text = gather_all(
        n, wq, wo, kv, partial_pairs.reshape(n, ROWS, -1)
    )
    text = text.reshape(partial_pairs.shape)
    scalars = patch_id.astype(jnp.int32).reshape(1)

    def run(state):
        return layer(
            scalars, mask_blocks, counts, state, modulation,
            wq, wo, wq_all, wo_all, kv, kv_rim, text,
        )

    first = run(hidden_in)
    inbox = lax.ppermute(first, "section", [(i, i + 1) for i in range(lax.axis_size("section") - 1)])
    result = run(jnp.where(section_id == 0, hidden_in, inbox))
    return result[None]


def solution(mesh):
    in_specs = (
        P(("groups", "patch"), None),
        P("groups", "patch"),
        P(None, "section", None, None),
        P("groups"),
        P("section", "patch", None),
        P("section", "patch", None),
        P("section", "patch", None),
        P("section", ("groups", "patch"), None),
        P(("groups", "patch"), None),
        P(("groups", "patch")),
    )
    out_specs = P("section", ("groups", "patch"), None)
    return jax.shard_map(local, mesh=mesh, in_specs=in_specs, out_specs=out_specs, check_vma=False)
```

time: 589 us -> 337 us (0.57)
  Pallas kernels: 0 us -> 319 us
  blocking collectives: 212 us -> 0 us
  waiting for transfers between devices: 180 us -> 6.45 us
  matrix products: 67.8 us -> 1.72 us
  local copies, waits for them, and re-layouts: 62.2 us -> 1.5 us
  other arithmetic: 37.3 us -> 5.03 us
  between operations: 14.2 us -> 0.85 us
  starting transfers between devices: 11.3 us -> 1.29 us
    pallas_call x0 -> x3, Pallas kernels: none -> 319 us  [the longest x1 247 us: gather_all(): pl.pallas_call(functools.partial(gather_kernel, n), out_shape=(jax.ShapeD...]
    psum x1 -> x0, blocking collectives: 212 us -> none  [local(): text_pairs = lax.psum(partial_pairs, 'patch').astype(jnp.bfloat16)]
    all_gather x2 -> x0, waiting for transfers between devices: 166 us -> none  [the longest x1 138 us: local(): lax.all_gather(w_out, 'patch', axis=1, tiled=True)]
    dot_general x12 -> x0, matrix products: 45.9 us -> none  [the longest x4 20.5 us: layer_block(): query = jnp.dot(normed, query_whole, preferred_element_type=jnp.float32)]
    gather x8 -> x0, local copies, waits for them, and re-layouts: 40.2 us -> none  [layer_block(): jnp.take(stale_blocks, chosen, axis=0).reshape(-1, stale_blocks.shape[2])]
    sub x4 -> x0, matrix products: 20.2 us -> none  [attend_block(): raised = jnp.exp(scores - peak)]
    concatenate x5 -> x0, other arithmetic: 18.1 us -> none  [the longest x4 11.6 us: attend_block(): joined = jnp.concatenate([text_pairs, image_pairs], axis=0)]
    while x41 -> x0, local copies, waits for them, and re-layouts: 14.3 us -> none
  transfers between devices with their start and end apart: 8 -> 1, of which waited for: 6 -> 1; matrix products, arithmetic and copies ran while one was open for 2% -> 0% of each run, Pallas kernels for 0% -> 0%
where the time goes in v1:
time: 337 us; the launch traced here: 336 us
  Pallas kernels  319 us (95%)
  waiting for transfers between devices  6.45 us (2%)
  other arithmetic  5.03 us (1%)
    pallas_call x1, Pallas kernels, gather_all(): pl.pallas_call(functools.partial(gather_kernel, n), out_shape=(jax.ShapeD...  247 us
    pallas_call x2, Pallas kernels, layer(): pl.pallas_call(layer_kernel, out_shape=jax.ShapeDtypeStruct(state.shape,...  72.3 us
  transfers between devices with their start and end apart: 1, of which 1 were waited for; matrix products, arithmetic and copies ran while one was open for 0% of the time, Pallas kernels for 0%

profile of v1, /device:TPU:5, one launch (start us, length us, event | category | flops | bytes accessed | tf_op | source)
XLA Modules:
  0.0 336.3 jit_solution(4724077780943353347)
XLA Ops:
  0.0 0.0 copy-start
  0.8 0.8 constant_dynamic-slice_fusion
  1.6 0.7 copy.13
  2.3 0.7 fusion.2
  3.0 0.9 add_convert_fusion
  3.9 0.0 copy-done
  4.0 1.7 fusion.part
  5.7 247.2 %gather_all.1 = (bf16[8,384,1536]{2,1,0:T(8,128)(2,1)}, bf16[8,192,3072]{2,1,0:T(8,128)(2,1)}, bf16[2,384,3072]{2,1,0:T(8,128)(2,1)}, bf16[8,16,3072]{2,1,0:T(8,128)(2,1)}) custom-call(bf16[384,1536]{1,0:T(8,128)(2,1)} %bitcast.22, bf16[192,3072]{1,0:T(8,128)(2,1)} %bitcast.25, bf16[384,3072]{1,0:T(8,128)(2,1)} %bitcast.19, f32[8,16,3072]{2,1,0:T(8,128)} %fusion.part), custom_call_target="tpu_custom_call" | custom-call | tf_op jit(solution)/shard_map/gather_all/pallas_call | solution.py:181
  252.9 36.1 %layer.2 = bf16[384,3072]{1,0:T(8,128)(2,1)} custom-call(s32[1]{0:T(128)} %bitcast.scalars, s32[3,4]{1,0:T(4,128)} %chosen.3, s32[3]{0:T(128)} %counts.3, bf16[384,3072]{1,0:T(8,128)(2,1)} %state.1, f32[5,3072]{1,0:T(8,128)} %bitcast.30, bf16[384,1536]{1,0:T(8,128)(2,1)} %bitcast.23, bf16[192,3072]{1,0:T(8,128)(2,1)} %bitcast.26, ...), custom_call_target="tpu_custom_call" | custom-call | tf_op jit(solution)/shard_map/layer/pallas_call | solution.py:334
  289.0 1.3 collective-permute-start
  290.3 6.4 %collective-permute-done = bf16[384,3072]{1,0:T(8,128)(2,1)} collective-permute-done((bf16[384,3072]{1,0:T(8,128)(2,1)}, bf16[384,3072]{1,0:T(8,128)(2,1)}, u32[]{:S(2)}, u32[]{:S(2)}) %collective-permute-start) | collective-permute-done | bytes 2359328 | tf_op jit(solution)/shard_map/ppermute | solution.py:381
  296.8 3.4 %broadcast_select_fusion.state = bf16[384,3072]{1,0:T(8,128)(2,1)} fusion(bf16[384,3072]{1,0:T(8,128)(2,1)} %state.1, bf16[384,3072]{1,0:T(8,128)(2,1)} %collective-permute-done, pred[]{:T(512)S(6)} %eq.3), kind=kLoop, calls=%fused_computation.2 | loop fusion | flops 1179648 | bytes 7077889 | tf_op jit(solution)/shard_map/jit(_where)/select_n | solution.py:382
  300.2 36.1 %layer.3 = bf16[384,3072]{1,0:T(8,128)(2,1)} custom-call(s32[1]{0:T(128)} %bitcast.scalars, s32[3,4]{1,0:T(4,128)} %chosen.3, s32[3]{0:T(128)} %counts.3, bf16[384,3072]{1,0:T(8,128)(2,1)} %broadcast_select_fusion.state, f32[5,3072]{1,0:T(8,128)} %bitcast.31, bf16[384,1536]{1,0:T(8,128)(2,1)} %bitcast.24, bf16[192,3072]{1,0:T(8,128)(2,1)} %bitcast.27, ...), custom_call_target="tpu_custom_call" | custom-call | tf_op jit(solution)/shard_map/layer/pallas_call | solution.py:334
Async XLA Ops:
  0.0 3.9 %copy-start = (bf16[1,384,3072]{2,1,0:T(8,128)(2,1)S(1)}, bf16[1,384,3072]{2,1,0:T(8,128)(2,1)}, u32[]{:S(2)}) copy-start(bf16[1,384,3072]{2,1,0:T(8,128)(2,1)} %param.16) | copy-start | bytes 7077892
  289.0 7.8 %collective-permute-start = (bf16[384,3072]{1,0:T(8,128)(2,1)}, bf16[384,3072]{1,0:T(8,128)(2,1)}, u32[]{:S(2)}, u32[]{:S(2)}) collective-permute-start(bf16[384,3072]{1,0:T(8,128)(2,1)} %layer.2), channel_id=1, source_target_pairs={{0,1},{2,3},{4,5},{6,7},{8,9},{10,11},{12,13},{14,15},{16,17},{18,... | collective-permute-start | bytes 7077896 | tf_op jit(solution)/shard_map/ppermute | solution.py:381

commit v2 on v0

v2 whole, which is shorter than its diff:
```python
import functools

import jax
import jax.numpy as jnp
from jax import lax
from jax.experimental import pallas as pl
from jax.experimental.pallas import tpu as pltpu
from jax.sharding import PartitionSpec as P

HD = 128
BLK = 128
EPSILON = 1e-06
MESH = pl.DeviceIdType.MESH
ROWS = 16


def exclusive_rows(rows):
    return max(rows * 5 // 12 // ROWS, 1) * ROWS


LAG = 2
TILE = 256


def kernel(
    n, chosen, counts, modulation, state, wq, wo, kv, part, out,
    wq_all, wo_all, kvs, text, sums, total, normed, query, mixed, inbox,
    ring_send, ring_recv, mate_send, mate_recv, rim_send, rim_recv,
    text_send, text_recv, share_send, share_recv, hand_send, hand_recv, own_sem, text_sem,
):
    me = lax.axis_index("patch")
    group = lax.axis_index("groups")
    section = lax.axis_index("section")
    parity = lax.rem(group, 2)
    mate = group + 1 - 2 * parity
    half = n // 2
    odd = lax.rem(me, 2)
    place = (1 - odd) * lax.div(me, 2) + odd * (n - 1 - lax.div(me, 2))
    tokens, width = state.shape
    inner = query.shape[1]
    heads = inner // HD
    blocks = kv.shape[0]
    chunks = part.shape[0]
    spread = chosen.shape[1]
    lead = text.shape[0]
    keys = lead + spread * BLK

    def at(position):
        position = lax.rem(position + n, n)
        high = lax.div(position, half)
        return (1 - high) * 2 * position + high * (2 * (n - 1 - position) + 1)

    def when(needed, condition, action):
        if needed:
            pl.when(condition)(action)
        else:
            action()

    right, left = at(place + 1), at(place - 1)

    own_copies = [
        pltpu.make_async_copy(wq, wq_all.at[pl.ds(pl.multiple_of(me * wq.shape[0], ROWS), wq.shape[0])], own_sem.at[0]),
        pltpu.make_async_copy(wo, wo_all.at[pl.ds(pl.multiple_of(me * wo.shape[0], ROWS), wo.shape[0])], own_sem.at[1]),
        pltpu.make_async_copy(kv, kvs.at[pl.ds(blocks, blocks)], own_sem.at[2]),
    ]

    barrier = pltpu.get_barrier_semaphore()
    for step in range(1, n):
        pl.semaphore_signal(barrier, inc=1, device_id={"patch": lax.rem(me + step, n)}, device_id_type=MESH)
    pl.semaphore_signal(barrier, inc=1, device_id={"groups": mate}, device_id_type=MESH)
    pl.semaphore_signal(barrier, inc=1, device_id={"section": 1 - section}, device_id_type=MESH)
    pl.semaphore_wait(barrier, n + 1)

    flows = (
        (wq, wq_all, -1, half),
        (wq, wq_all, 1, half - 1),
        (wo, wo_all, -1, half - 1),
        (wo, wo_all, 1, half),
    )

    def remote(src, dst, send, recv, target):
        return pltpu.make_async_remote_copy(
            src_ref=src, dst_ref=dst, send_sem=send, recv_sem=recv,
            device_id=target, device_id_type=MESH,
        )

    def span(start, size):
        return pl.ds(pl.multiple_of(start, ROWS), size)

    def ring(flow, hop, received=False):
        own, every, way, _ = flows[flow]
        rows = own.shape[0]
        apart = exclusive_rows(rows)
        keep = rows - apart
        shard = at(place + way * (hop if received else hop - 1))
        dst = every.at[span(shard * rows + parity * apart, keep)]
        src = own.at[span(parity * apart, keep)] if hop == 1 and not received else dst
        target = {"patch": right if way < 0 else left}
        return remote(src, dst, ring_send.at[flow, hop - 1], ring_recv.at[flow, hop - 1], target)

    def across(flow, hop, received=False):
        own, every, way, _ = flows[flow]
        rows = own.shape[0]
        apart = exclusive_rows(rows)
        keep = rows - apart
        shard = at(place + way * hop)
        side = 1 - parity if received else parity
        ref = every.at[span(shard * rows + side * keep, apart)]
        return remote(ref, ref, mate_send.at[flow, hop - 1], mate_recv.at[flow, hop - 1], {"groups": mate})

    def rim(side, block):
        return remote(
            kv.at[block], kvs.at[2 * side * blocks + block],
            rim_send.at[side, block], rim_recv.at[side, block],
            {"patch": me + 1 if side == 0 else me - 1},
        )

    def rim_start(block):
        pl.when(me < n - 1)(lambda: rim(0, block).start())
        pl.when(me > 0)(lambda: rim(1, block).start())

    few = chunks < n

    def scatter(step, received=False):
        peer = lax.rem(me + step, n)
        source = lax.rem(me + n - step, n)
        return remote(
            part.at[jnp.minimum(peer, chunks - 1) if few else peer], sums.at[source if received else me],
            text_send.at[step - 1], text_recv.at[step - 1], {"patch": peer},
        )

    def share(step, received=False):
        peer = lax.rem(me + step, n)
        slot = lax.rem(me + n - step, n) if received else me
        ref = text.at[span((jnp.minimum(slot, chunks - 1) if few else slot) * ROWS, ROWS)]
        return remote(ref, ref, share_send.at[step - 1], share_recv.at[step - 1], {"patch": peer})

    own_chunk = jnp.minimum(me, chunks - 1) if few else me
    own_sum = pltpu.make_async_copy(part.at[own_chunk], sums.at[me], text_sem.at[0])
    keep_sum = pltpu.make_async_copy(total, text.at[span(own_chunk * ROWS, ROWS)], text_sem.at[1])

    def text_start():
        when(few, me < chunks, own_sum.start)
        for step in range(1, n):
            when(few, lax.rem(me + step, n) < chunks, scatter(step).start)

    def text_reduce():
        def reduce():
            own_sum.wait()
            for step in range(1, n):
                scatter(step, True).wait_recv()
            total[...] = jnp.sum(sums[...], axis=0).astype(total.dtype)
            keep_sum.start()
            keep_sum.wait()
            for step in range(1, n):
                share(step).start()

        when(few, me < chunks, reduce)

    def text_arrive():
        for step in range(1, n):
            when(few, lax.rem(me + n - step, n) < chunks, share(step, True).wait_recv)

    def norm(source):
        step = ROWS

        @pl.loop(0, tokens // step)
        def _(index):
            window = pl.ds(pl.multiple_of(index * step, step), step)
            values = source[window, :].astype(jnp.float32)
            center = values - jnp.mean(values, axis=-1, keepdims=True)
            variance = jnp.mean(center * center, axis=-1, keepdims=True)
            scaled = center * lax.rsqrt(variance + EPSILON)
            normed[window, :] = (
                scaled * (1.0 + modulation[1:2, :]) + modulation[0:1, :]
            ).astype(normed.dtype)

    def project_query():
        @pl.loop(0, inner // TILE)
        def _(index):
            window = pl.ds(pl.multiple_of(index * TILE, TILE), TILE)
            query[:, window] = jnp.dot(
                normed[...], wq_all[:, window], preferred_element_type=jnp.float32
            ).astype(query.dtype)

    together = 4 if heads % 4 == 0 else 1

    def attend(first, last):
        bunches = heads // together

        @pl.loop(first * bunches, last * bunches)
        def _(index):
            block = lax.div(index, bunches)
            bunch = lax.rem(index, bunches)
            rows = pl.ds(pl.multiple_of(block * BLK, BLK), BLK)
            limit = lead + counts[block] * BLK
            live = lax.broadcasted_iota(jnp.int32, (BLK, keys), 1) < limit
            picks = [
                jnp.clip(chosen[block, slot] - (me - 1) * blocks, 0, 3 * blocks - 1)
                for slot in range(spread)
            ]
            for one in range(together):
                start = bunch * (together * HD) + one * HD
                columns = pl.ds(pl.multiple_of(start, HD), HD)
                beyond = pl.ds(pl.multiple_of(inner + start, HD), HD)
                key = jnp.concatenate([text[:, columns]] + [kvs[pick, :, columns] for pick in picks], axis=0)
                value = jnp.concatenate([text[:, beyond]] + [kvs[pick, :, beyond] for pick in picks], axis=0)
                scores = lax.dot_general(
                    query[rows, columns], key, (((1,), (1,)), ((), ())),
                    preferred_element_type=jnp.float32,
                )
                scores = jnp.where(live, scores, -1e30)
                peak = jnp.max(scores, axis=-1, keepdims=True)
                raised = jnp.exp((scores - peak) * HD ** (-0.5))
                whole = jnp.sum(raised, axis=-1, keepdims=True)
                share_of = jnp.dot(
                    raised.astype(jnp.bfloat16), value, preferred_element_type=jnp.float32
                )
                mixed[rows, columns] = (share_of / whole).astype(mixed.dtype)

    parts = width // (3 * TILE) if width % (3 * TILE) == 0 else 1
    part_width = width // parts

    def project_out(source, index_from, index_to):
        @pl.loop(index_from, index_to)
        def _(index):
            window = pl.ds(pl.multiple_of(index * TILE, TILE), TILE)
            projected = jnp.dot(mixed[...], wo_all[:, window], preferred_element_type=jnp.float32)
            out[:, window] = (
                source[:, window].astype(jnp.float32) + modulation[2:3, window] * projected
            ).astype(out.dtype)

    def hand(index):
        window = pl.ds(index * part_width, part_width)
        return remote(
            out.at[:, window], inbox.at[:, window],
            hand_send.at[index], hand_recv.at[index], {"section": 1 - section},
        )

    def relay(flow, hop):
        if hop <= flows[flow][3]:
            ring(flow, hop, True).wait_recv()
            if hop < flows[flow][3]:
                ring(flow, hop + 1).start()
            across(flow, hop).start()

    ring(0, 1).start()
    ring(1, 1).start()
    text_start()
    for copy in own_copies:
        copy.start()
    rim_start(0)
    started = 1
    pl.when(section == 0)(lambda: norm(state))
    for hop in range(1, half + 1):
        relay(0, hop)
        relay(1, hop)
        if hop == max(LAG - 1, 1):
            ring(2, 1).start()
            ring(3, 1).start()
        if hop > LAG:
            relay(2, hop - LAG)
            relay(3, hop - LAG)
        if hop == 1:
            text_reduce()
        if started < blocks:
            rim_start(started)
            started += 1
    for block in range(started, blocks):
        rim_start(block)

    def wait_query():
        for flow in range(2):
            for hop in range(1, flows[flow][3] + 1):
                across(flow, hop, True).wait_recv()
        own_copies[0].wait()

    def wait_keys():
        own_copies[2].wait()
        for block in range(blocks):
            pl.when(me < n - 1)(lambda: rim(1, block).wait_recv())
            pl.when(me > 0)(lambda: rim(0, block).wait_recv())
        text_arrive()

    todo = [h for h in range(half - LAG + 1, half + 1)]

    def relay_next():
        if todo:
            hop = todo.pop(0)
            relay(2, hop)
            relay(3, hop)

    wait_query()
    pl.when(section == 0)(project_query)
    relay_next()
    wait_keys()
    for block in range(blocks):
        pl.when(section == 0)(lambda: attend(block, block + 1))
        relay_next()
    while todo:
        relay_next()
    for flow in range(2, 4):
        for hop in range(1, flows[flow][3] + 1):
            across(flow, hop, True).wait_recv()
    own_copies[1].wait()

    each = part_width // TILE

    @pl.when(section == 0)
    def _():
        for index in range(parts):
            project_out(state, index * each, (index + 1) * each)
            if index:
                hand(index - 1).start()
        hand(parts - 1).start()

    @pl.when(section == 1)
    def _():
        for index in range(parts):
            hand(index).wait_recv()
        norm(inbox)
        project_query()
        attend(0, blocks)
        project_out(inbox, 0, width // TILE)

    for flow in range(4):
        for hop in range(1, flows[flow][3] + 1):
            across(flow, hop).wait_send()
            ring(flow, hop).wait_send()
    for step in range(1, n):
        when(few, lax.rem(me + step, n) < chunks, scatter(step).wait_send)
        when(few, me < chunks, share(step).wait_send)
    for block in range(blocks):
        pl.when(me < n - 1)(lambda: rim(0, block).wait_send())
        pl.when(me > 0)(lambda: rim(1, block).wait_send())

    @pl.when(section == 0)
    def _():
        for index in range(parts):
            hand(index).wait_send()


def run(n, chosen, counts, modulation, state, wq, wo, kv, part):
    half = n // 2
    tokens, width = state.shape
    inner = wq.shape[1]
    blocks = kv.shape[0]
    smem = pl.BlockSpec(memory_space=pltpu.SMEM)
    vmem = pl.BlockSpec(memory_space=pltpu.VMEM)
    anywhere = pl.BlockSpec(memory_space=pl.ANY)
    dma = pltpu.SemaphoreType.DMA
    parts = width // (3 * TILE) if width % (3 * TILE) == 0 else 1
    b16 = jnp.bfloat16
    return pl.pallas_call(
        functools.partial(kernel, n),
        out_shape=jax.ShapeDtypeStruct(state.shape, state.dtype),
        in_specs=[smem, smem, vmem, vmem] + [anywhere] * 4,
        out_specs=vmem,
        scratch_shapes=[
            pltpu.VMEM((n * wq.shape[0], inner), b16),
            pltpu.VMEM((n * wo.shape[0], width), b16),
            pltpu.VMEM((3 * blocks,) + kv.shape[1:], b16),
            pltpu.VMEM((part.shape[0] * ROWS, kv.shape[2]), b16),
            pltpu.VMEM((n,) + part.shape[1:], jnp.float32),
            pltpu.VMEM(part.shape[1:], b16),
            pltpu.VMEM((tokens, width), b16),
            pltpu.VMEM((tokens, inner), b16),
            pltpu.VMEM((tokens, inner), b16),
            pltpu.VMEM((tokens, width), b16),
            dma((4, half)), dma((4, half)), dma((4, half)), dma((4, half)),
            dma((2, blocks)), dma((2, blocks)),
            dma((n - 1,)), dma((n - 1,)), dma((n - 1,)), dma((n - 1,)),
            dma((parts,)), dma((parts,)), dma((3,)), dma((2,)),
        ],
        compiler_params=pltpu.CompilerParams(
            collective_id=0, has_side_effects=True, vmem_limit_bytes=60 * 2**20
        ),
        name="layers",
    )(chosen, counts, modulation, state, wq, wo, kv, part)


def local(
    hidden_in, text_rows, mod_table, timestep, w_query, w_out, w_text, stale_kv, mask_blocks, counts
):
    patch_id = lax.axis_index("patch")
    n = lax.axis_size("patch")
    width = text_rows.shape[1]
    modulation = lax.dynamic_index_in_dim(mod_table, timestep[0], 0, keepdims=False)[0]
    text_shift = lax.dynamic_slice_in_dim(modulation[3], patch_id * width, width, 0)
    text_scale = lax.dynamic_slice_in_dim(modulation[4], patch_id * width, width, 0)
    conditioned = (text_rows.astype(jnp.float32) * (1.0 + text_scale) + text_shift).astype(
        jnp.bfloat16
    )
    partial_pairs = jnp.dot(conditioned, w_text[0], preferred_element_type=jnp.float32)
    kv = stale_kv[0].reshape(-1, BLK, stale_kv.shape[2])
    part = partial_pairs.reshape(-1, ROWS, partial_pairs.shape[1])
    result = run(n, mask_blocks, counts, modulation, hidden_in, w_query[0], w_out[0], kv, part)
    return result[None]


def solution(mesh):
    in_specs = (
        P(("groups", "patch"), None),
        P("groups", "patch"),
        P(None, "section", None, None),
        P("groups"),
        P("section", "patch", None),
        P("section", "patch", None),
        P("section", "patch", None),
        P("section", ("groups", "patch"), None),
        P(("groups", "patch"), None),
        P(("groups", "patch")),
    )
    out_specs = P("section", ("groups", "patch"), None)
    return jax.shard_map(local, mesh=mesh, in_specs=in_specs, out_specs=out_specs, check_vma=False)
```

time: 589 us -> 322 us (0.55)
  Pallas kernels: 0 us -> 313 us
  blocking collectives: 212 us -> 0 us
  waiting for transfers between devices: 180 us -> 0 us
  matrix products: 67.8 us -> 1.72 us
  local copies, waits for them, and re-layouts: 62.2 us -> 4.72 us
  other arithmetic: 37.3 us -> 1.64 us
  between operations: 14.2 us -> 0.83 us
  starting transfers between devices: 11.3 us -> 0 us
    pallas_call x0 -> x1, Pallas kernels: none -> 313 us  [run(): pl.pallas_call(functools.partial(kernel, n), out_shape=jax.ShapeDtypeStru...]
    psum x1 -> x0, blocking collectives: 212 us -> none  [local(): text_pairs = lax.psum(partial_pairs, 'patch').astype(jnp.bfloat16)]
    all_gather x2 -> x0, waiting for transfers between devices: 166 us -> none  [the longest x1 138 us: local(): lax.all_gather(w_out, 'patch', axis=1, tiled=True)]
    dot_general x12 -> x0, matrix products: 45.9 us -> none  [the longest x4 20.5 us: layer_block(): query = jnp.dot(normed, query_whole, preferred_element_type=jnp.float32)]
    gather x8 -> x0, local copies, waits for them, and re-layouts: 40.2 us -> none  [layer_block(): jnp.take(stale_blocks, chosen, axis=0).reshape(-1, stale_blocks.shape[2])]
    sub x4 -> x0, matrix products: 20.2 us -> none  [attend_block(): raised = jnp.exp(scores - peak)]
    concatenate x5 -> x0, other arithmetic: 18.1 us -> none  [the longest x4 11.6 us: attend_block(): joined = jnp.concatenate([text_pairs, image_pairs], axis=0)]
    while x41 -> x0, local copies, waits for them, and re-layouts: 14.3 us -> none
  transfers between devices with their start and end apart: 8 -> 0, of which waited for: 6 -> 0; matrix products, arithmetic and copies ran while one was open for 2% -> 0% of each run, Pallas kernels for 0% -> 0%
where the time goes in v2:
time: 322 us
  Pallas kernels  313 us (97%)
  local copies, waits for them, and re-layouts  4.72 us (1%)
    pallas_call x1, Pallas kernels, run(): pl.pallas_call(functools.partial(kernel, n), out_shape=jax.ShapeDtypeStru...  313 us

profile of v2, /device:TPU:5, one launch (start us, length us, event | category | flops | bytes accessed | tf_op | source)
XLA Modules:
  0.0 321.9 jit_solution(11092540551027451933)
XLA Ops:
  0.0 0.0 copy-start
  0.8 0.7 fusion.2
  1.5 0.8 constant_dynamic-slice_fusion
  2.4 0.7 copy.13
  3.0 0.9 add_convert_fusion
  3.9 0.0 copy-done
  4.0 1.7 fusion.part
  5.7 313.0 %layers.1 = bf16[384,3072]{1,0:T(8,128)(2,1)} custom-call(s32[3,4]{1,0:T(4,128)} %chosen.1, s32[3]{0:T(128)} %counts.1, f32[5,3072]{1,0:T(8,128)} %bitcast.22, bf16[384,3072]{1,0:T(8,128)(2,1)} %state.1, bf16[384,1536]{1,0:T(8,128)(2,1)} %bitcast.19, bf16[192,3072]{1,0:T(8,128)(2,1)} %bitcast.20, bf16[3,128,3072]{2,1,0:T(8,128)(2,1)} %bitcast.18, ...), custom_call_target="tpu_custom_call" | custom-call | tf_op jit(solution)/shard_map/layers/pallas_call | solution.py:354
  318.7 3.2 %copy.16 = bf16[1,384,3072]{2,1,0:T(8,128)(2,1)} copy(bf16[1,384,3072]{2,1,0:T(8,128)(2,1)} %bitcast.17) | data formatting | bytes 4718592
Async XLA Ops:
  0.0 4.0 %copy-start = (bf16[1,384,3072]{2,1,0:T(8,128)(2,1)S(1)}, bf16[1,384,3072]{2,1,0:T(8,128)(2,1)}, u32[]{:S(2)}) copy-start(bf16[1,384,3072]{2,1,0:T(8,128)(2,1)} %param.16) | copy-start | bytes 7077892

commit v3 on v2

--- a/solution.py
+++ b/solution.py
@@ -18,7 +18,7 @@
     return max(rows * 5 // 12 // ROWS, 1) * ROWS
 
 
-LAG = 2
+LAG = 0
 TILE = 256
 
 
@@ -108,16 +108,26 @@
         ref = every.at[span(shard * rows + side * keep, apart)]
         return remote(ref, ref, mate_send.at[flow, hop - 1], mate_recv.at[flow, hop - 1], {"groups": mate})
 
-    def rim(side, block):
+    pair = me + 1 - 2 * odd
+    onward, behind = me + 2 - 4 * odd, me - 2 + 4 * odd
+    has_onward = (onward >= 0) & (onward < n)
+    has_behind = (behind >= 0) & (behind < n)
+
+    def rim(leg, block, received=False):
+        near, far = 2 * (1 - odd) * blocks + block, 2 * odd * blocks + block
+        if received:
+            dst = kvs.at[far if leg else near]
+        else:
+            dst = kvs.at[far]
+        src = kvs.at[near] if leg else kv.at[block]
         return remote(
-            kv.at[block], kvs.at[2 * side * blocks + block],
-            rim_send.at[side, block], rim_recv.at[side, block],
-            {"patch": me + 1 if side == 0 else me - 1},
+            src, dst, rim_send.at[leg, block], rim_recv.at[leg, block],
+            {"patch": onward if leg else pair},
         )
 
-    def rim_start(block):
-        pl.when(me < n - 1)(lambda: rim(0, block).start())
-        pl.when(me > 0)(lambda: rim(1, block).start())
+    def rim_forward(block):
+        rim(0, block, True).wait_recv()
+        pl.when(has_onward)(lambda: rim(1, block).start())
 
     few = chunks < n
 
@@ -149,7 +159,7 @@
             own_sum.wait()
             for step in range(1, n):
                 scatter(step, True).wait_recv()
-            total[...] = jnp.sum(sums[...], axis=0).astype(total.dtype)
+            total[...] = jnp.sum(sums[...].astype(jnp.float32), axis=0).astype(total.dtype)
             keep_sum.start()
             keep_sum.wait()
             for step in range(1, n):
@@ -247,27 +257,31 @@
     ring(0, 1).start()
     ring(1, 1).start()
     text_start()
+    if LAG < 2:
+        ring(2, 1).start()
+        ring(3, 1).start()
     for copy in own_copies:
         copy.start()
-    rim_start(0)
-    started = 1
+    for block in range(blocks):
+        rim(0, block).start()
+    forwarded = 0
     pl.when(section == 0)(lambda: norm(state))
     for hop in range(1, half + 1):
         relay(0, hop)
         relay(1, hop)
-        if hop == max(LAG - 1, 1):
+        if hop == LAG - 1:
             ring(2, 1).start()
             ring(3, 1).start()
         if hop > LAG:
             relay(2, hop - LAG)
             relay(3, hop - LAG)
-        if hop == 1:
+        if hop == max(half - 1, 1):
             text_reduce()
-        if started < blocks:
-            rim_start(started)
-            started += 1
-    for block in range(started, blocks):
-        rim_start(block)
+        if 2 <= hop and forwarded < blocks:
+            rim_forward(forwarded)
+            forwarded += 1
+    for block in range(forwarded, blocks):
+        rim_forward(block)
 
     def wait_query():
         for flow in range(2):
@@ -278,8 +292,7 @@
     def wait_keys():
         own_copies[2].wait()
         for block in range(blocks):
-            pl.when(me < n - 1)(lambda: rim(1, block).wait_recv())
-            pl.when(me > 0)(lambda: rim(0, block).wait_recv())
+            pl.when(has_behind)(lambda: rim(1, block, True).wait_recv())
         text_arrive()
 
     todo = [h for h in range(half - LAG + 1, half + 1)]
@@ -331,8 +344,8 @@
         when(few, lax.rem(me + step, n) < chunks, scatter(step).wait_send)
         when(few, me < chunks, share(step).wait_send)
     for block in range(blocks):
-        pl.when(me < n - 1)(lambda: rim(0, block).wait_send())
-        pl.when(me > 0)(lambda: rim(1, block).wait_send())
+        rim(0, block).wait_send()
+        pl.when(has_onward)(lambda: rim(1, block).wait_send())
 
     @pl.when(section == 0)
     def _():
@@ -361,7 +374,7 @@
             pltpu.VMEM((n * wo.shape[0], width), b16),
             pltpu.VMEM((3 * blocks,) + kv.shape[1:], b16),
             pltpu.VMEM((part.shape[0] * ROWS, kv.shape[2]), b16),
-            pltpu.VMEM((n,) + part.shape[1:], jnp.float32),
+            pltpu.VMEM((n,) + part.shape[1:], part.dtype),
             pltpu.VMEM(part.shape[1:], b16),
             pltpu.VMEM((tokens, width), b16),
             pltpu.VMEM((tokens, inner), b16),
@@ -392,6 +405,7 @@
         jnp.bfloat16
     )
     partial_pairs = jnp.dot(conditioned, w_text[0], preferred_element_type=jnp.float32)
+    partial_pairs = partial_pairs.astype(jnp.bfloat16)
     kv = stale_kv[0].reshape(-1, BLK, stale_kv.shape[2])
     part = partial_pairs.reshape(-1, ROWS, partial_pairs.shape[1])
     result = run(n, mask_blocks, counts, modulation, hidden_in, w_query[0], w_out[0], kv, part)

time: 322 us -> 281 us (0.87)
  the two profiles are of different devices: /device:TPU:5 before, /device:TPU:9 now
where the time goes in v3:
time: 281 us
  Pallas kernels  272 us (97%)
  local copies, waits for them, and re-layouts  4.72 us (2%)
    pallas_call x1, Pallas kernels, run(): pl.pallas_call(functools.partial(kernel, n), out_shape=jax.ShapeDtypeStru...  272 us

profile of v3, /device:TPU:9, one launch (start us, length us, event | category | flops | bytes accessed | tf_op | source)
XLA Modules:
  0.0 280.8 jit_solution(5177799082406148173)
XLA Ops:
  0.0 0.0 copy-start
  0.8 0.7 fusion.3
  1.5 0.8 constant_dynamic-slice_fusion
  2.4 0.7 copy.13
  3.0 0.0 copy-done
  3.0 2.4 convolution_convert_fusion
  5.4 272.2 %layers.1 = bf16[384,3072]{1,0:T(8,128)(2,1)} custom-call(s32[3,4]{1,0:T(4,128)} %chosen.1, s32[3]{0:T(128)} %counts.1, f32[5,3072]{1,0:T(8,128)} %bitcast.20, bf16[384,3072]{1,0:T(8,128)(2,1)} %state.1, bf16[384,1536]{1,0:T(8,128)(2,1)} %bitcast.18, bf16[192,3072]{1,0:T(8,128)(2,1)} %bitcast.19, bf16[3,128,3072]{2,1,0:T(8,128)(2,1)} %bitcast.17, ...), custom_call_target="tpu_custom_call" | custom-call | tf_op jit(solution)/shard_map/layers/pallas_call | solution.py:367
  277.6 3.2 %copy.16 = bf16[1,384,3072]{2,1,0:T(8,128)(2,1)} copy(bf16[1,384,3072]{2,1,0:T(8,128)(2,1)} %bitcast.15) | data formatting | bytes 4718592
Async XLA Ops:
  0.0 3.0 %copy-start = (bf16[1,384,3072]{2,1,0:T(8,128)(2,1)S(1)}, bf16[1,384,3072]{2,1,0:T(8,128)(2,1)}, u32[]{:S(2)}) copy-start(bf16[1,384,3072]{2,1,0:T(8,128)(2,1)} %param.16) | copy-start | bytes 7077892

commit v4 on v3

--- a/solution.py
+++ b/solution.py
@@ -262,8 +262,11 @@
         ring(3, 1).start()
     for copy in own_copies:
         copy.start()
-    for block in range(blocks):
-        rim(0, block).start()
+    def rim_start():
+        for block in range(blocks):
+            rim(0, block).start()
+
+    pl.when(section == 0)(rim_start)
     forwarded = 0
     pl.when(section == 0)(lambda: norm(state))
     for hop in range(1, half + 1):
@@ -278,10 +281,11 @@
         if hop == max(half - 1, 1):
             text_reduce()
         if 2 <= hop and forwarded < blocks:
-            rim_forward(forwarded)
+            pl.when(section == 0)(lambda: rim_forward(forwarded))
             forwarded += 1
     for block in range(forwarded, blocks):
-        rim_forward(block)
+        pl.when(section == 0)(lambda: rim_forward(block))
+    pl.when(section == 1)(rim_start)
 
     def wait_query():
         for flow in range(2):
@@ -306,12 +310,17 @@
     wait_query()
     pl.when(section == 0)(project_query)
     relay_next()
-    wait_keys()
+    pl.when(section == 0)(wait_keys)
     for block in range(blocks):
         pl.when(section == 0)(lambda: attend(block, block + 1))
         relay_next()
     while todo:
         relay_next()
+    @pl.when(section == 1)
+    def _():
+        for block in range(blocks):
+            rim_forward(block)
+
     for flow in range(2, 4):
         for hop in range(1, flows[flow][3] + 1):
             across(flow, hop, True).wait_recv()
@@ -333,6 +342,7 @@
             hand(index).wait_recv()
         norm(inbox)
         project_query()
+        wait_keys()
         attend(0, blocks)
         project_out(inbox, 0, width // TILE)
 

time: 281 us -> 258 us (0.918)
  Pallas kernels: 272 us -> 249 us
    pallas_call x1, Pallas kernels: 272 us -> 249 us  [run(): pl.pallas_call(functools.partial(kernel, n), out_shape=jax.ShapeDtypeStru...]
where the time goes in v4:
time: 258 us
  Pallas kernels  249 us (97%)
  local copies, waits for them, and re-layouts  4.72 us (2%)
    pallas_call x1, Pallas kernels, run(): pl.pallas_call(functools.partial(kernel, n), out_shape=jax.ShapeDtypeStru...  249 us

profile of v4, /device:TPU:9, one launch (start us, length us, event | category | flops | bytes accessed | tf_op | source)
XLA Modules:
  0.0 257.7 jit_solution(9452069437692577926)
XLA Ops:
  0.0 0.0 copy-start
  0.8 0.7 fusion.3
  1.5 0.8 constant_dynamic-slice_fusion
  2.4 0.7 copy.13
  3.0 0.0 copy-done
  3.0 2.4 convolution_convert_fusion
  5.4 249.1 %layers.1 = bf16[384,3072]{1,0:T(8,128)(2,1)} custom-call(s32[3,4]{1,0:T(4,128)} %chosen.1, s32[3]{0:T(128)} %counts.1, f32[5,3072]{1,0:T(8,128)} %bitcast.20, bf16[384,3072]{1,0:T(8,128)(2,1)} %state.1, bf16[384,1536]{1,0:T(8,128)(2,1)} %bitcast.18, bf16[192,3072]{1,0:T(8,128)(2,1)} %bitcast.19, bf16[3,128,3072]{2,1,0:T(8,128)(2,1)} %bitcast.17, ...), custom_call_target="tpu_custom_call" | custom-call | tf_op jit(solution)/shard_map/layers/pallas_call | solution.py:377
  254.5 3.2 %copy.16 = bf16[1,384,3072]{2,1,0:T(8,128)(2,1)} copy(bf16[1,384,3072]{2,1,0:T(8,128)(2,1)} %bitcast.15) | data formatting | bytes 4718592
Async XLA Ops:
  0.0 3.0 %copy-start = (bf16[1,384,3072]{2,1,0:T(8,128)(2,1)S(1)}, bf16[1,384,3072]{2,1,0:T(8,128)(2,1)}, u32[]{:S(2)}) copy-start(bf16[1,384,3072]{2,1,0:T(8,128)(2,1)} %param.16) | copy-start | bytes 7077892
